TPU v7x, 32 devices: a whole 2x2x4 slice. The times are simulated.
32 devices in a mesh: blk: 8 (over z, x), head: 4 (over y, core).
Axes of the slice: x: 2, y: 2, z: 4, core: 2. Of those that a mesh axis runs over, the one named last changes fastest.
Arguments:
- queries: bfloat16 [4096, 1024], P(('blk', 'head')), may hold values from -6 to 6
- key_vectors: bfloat16 [4096, 1024], P(('blk', 'head')), may hold values from -6 to 6
- value_vectors: bfloat16 [4096, 1024], P(('blk', 'head')), may hold values from -6 to 6
- grad_output: bfloat16 [4096, 1024], P(('blk', 'head')), may hold values from -6 to 6
- lengths: int32 [4], replicated, may hold values from 1 to 2048, 4096 in all
Outputs:
- grad_queries: bfloat16 [4096, 1024], P(('blk', 'head'))
- grad_keys: bfloat16 [4096, 1024], P(('blk', 'head'))
- grad_values: bfloat16 [4096, 1024], P(('blk', 'head'))
Inputs may be any that keep to these rules, and one draw needn't show every extreme that they name: 4 positive lengths that sum to 4096; the longest is exactly 2048.
All inputs are finite; a program needn't handle non-finite values.
Results may differ from a plain program's by a relative error of at most 0.0086.
Values may be sent and summed in bfloat16 or wider, within the bound.
No kernel may reach another device: no remote copies, remote signals or barrier semaphores. Data moves between devices by JAX's collectives and lax.ppermute only.
A program may use at most 64 MiB of HBM per device.

v0:
```python
import jax
import jax.numpy as jnp
from jax import lax
from jax.sharding import PartitionSpec as P

DH = 64
WIN = 64


def with_halo(block, sides, width):
    for axis, dim in sides:
        count = lax.axis_size(axis)
        forward = [(i, i + 1) for i in range(count - 1)]
        backward = [(target, source) for source, target in forward]
        low = lax.ppermute(
            lax.slice_in_dim(block, block.shape[dim] - width, None, axis=dim), axis, forward
        )
        high = lax.ppermute(lax.slice_in_dim(block, 0, width, axis=dim), axis, backward)
        block = jnp.concatenate([low, block, high], axis=dim)
    return block


def shifted(block, axis, distance):
    devices = range(lax.axis_size(axis))
    route = [(i - distance, i) for i in devices if i - distance in devices]
    return lax.ppermute(block, axis, route)


def recording_of(positions, rec_ends):
    return jnp.sum((rec_ends[None, :] <= positions[:, None]).astype(jnp.int32), axis=1)


def band_grads(query_rows, grad_rows, key_value, query_first, key_first, rec_ends, frames):
    row_count = query_rows.shape[0]
    columns = query_rows.shape[1]
    head_count = columns // DH
    step_rows = min(512, 2 * WIN)
    key_span = step_rows + 2 * WIN
    score_scale = DH ** (-0.5)
    pair_grad = jnp.zeros((key_value.shape[0], 2 * columns), jnp.float32)
    query_parts = []
    for first_row in range(0, row_count, step_rows):
        query_block = query_rows[first_row : first_row + step_rows].reshape(
            step_rows, head_count, DH
        )
        grad_block = grad_rows[first_row : first_row + step_rows].reshape(step_rows, head_count, DH)
        pair_block = key_value[first_row : first_row + key_span]
        key_block = pair_block[:, :columns].reshape(key_span, head_count, DH)
        value_block = pair_block[:, columns:].reshape(key_span, head_count, DH)
        query_pos = query_first + first_row + jnp.arange(step_rows, dtype=jnp.int32)
        key_pos = key_first + first_row + jnp.arange(key_span, dtype=jnp.int32)
        inside = (key_pos >= 0) & (key_pos < frames)
        visible = jnp.abs(query_pos[:, None] - key_pos[None, :]) <= WIN
        visible = visible & (
            recording_of(query_pos, rec_ends)[:, None] == recording_of(key_pos, rec_ends)[None, :]
        )
        visible = visible & (inside[None, :] | (query_pos[:, None] == key_pos[None, :]))
        scores = (
            jnp.einsum("qhd,khd->hqk", query_block, key_block, preferred_element_type=jnp.float32)
            * score_scale
        )
        scores = jnp.where(visible[None], scores, -1e30)
        row_max = jnp.max(scores, axis=-1, keepdims=True)
        weights = jnp.where(visible[None], jnp.exp(scores - row_max), 0.0)
        probs = weights / jnp.sum(weights, axis=-1, keepdims=True)
        probs_low = probs.astype(jnp.bfloat16)
        value_part = jnp.einsum(
            "hqk,qhd->khd", probs_low, grad_block, preferred_element_type=jnp.float32
        )
        prob_grad = jnp.einsum(
            "qhd,khd->hqk", grad_block, value_block, preferred_element_type=jnp.float32
        )
        row_delta = jnp.sum(probs * prob_grad, axis=-1, keepdims=True)
        score_grad = (probs * (prob_grad - row_delta) * score_scale).astype(jnp.bfloat16)
        query_grad = jnp.einsum(
            "hqk,khd->qhd", score_grad, key_block, preferred_element_type=jnp.float32
        )
        key_part = jnp.einsum(
            "hqk,qhd->khd", score_grad, query_block, preferred_element_type=jnp.float32
        )
        both_parts = jnp.concatenate(
            [key_part.reshape(key_span, columns), value_part.reshape(key_span, columns)], axis=1
        )
        pair_grad = pair_grad.at[first_row : first_row + key_span].add(both_parts)
        query_parts.append(query_grad.reshape(step_rows, columns))
    return (jnp.concatenate(query_parts, axis=0), pair_grad)


def body(queries, key_vectors, value_vectors, grad_output, lengths):
    group_size = lax.axis_size("head")
    block_rows = queries.shape[0] * group_size
    columns = queries.shape[1] // group_size
    frames = block_rows * lax.axis_size("blk")
    head_queries, head_keys, head_values, head_grads = (
        lax.all_to_all(queries, "head", split_axis=1, concat_axis=0, tiled=True),
        lax.all_to_all(key_vectors, "head", split_axis=1, concat_axis=0, tiled=True),
        lax.all_to_all(value_vectors, "head", split_axis=1, concat_axis=0, tiled=True),
        lax.all_to_all(grad_output, "head", split_axis=1, concat_axis=0, tiled=True),
    )
    key_value = jnp.concatenate([head_keys, head_values], axis=1)
    rec_ends = jnp.cumsum(lengths)
    base_pos = lax.axis_index("blk") * block_rows
    extended = with_halo(key_value, (("blk", 0),), WIN)
    query_grad, pair_grad = band_grads(
        head_queries, head_grads, extended, base_pos, base_pos - WIN, rec_ends, frames
    )
    own_rows = pair_grad[WIN : WIN + block_rows]
    arrived = []
    for step_by, rim_rows in ((1, pair_grad[WIN + block_rows :]), (-1, pair_grad[:WIN])):
        arrived.append(shifted(rim_rows, "blk", step_by))
    own_rows = own_rows.at[:WIN].add(arrived[0]).at[block_rows - WIN :].add(arrived[1])
    outputs = (
        lax.all_to_all(
            query_grad.astype(jnp.bfloat16), "head", split_axis=0, concat_axis=1, tiled=True
        ),
        lax.all_to_all(
            own_rows[:, :columns].astype(jnp.bfloat16),
            "head",
            split_axis=0,
            concat_axis=1,
            tiled=True,
        ),
        lax.all_to_all(
            own_rows[:, columns:].astype(jnp.bfloat16),
            "head",
            split_axis=0,
            concat_axis=1,
            tiled=True,
        ),
    )
    return (outputs[0], outputs[1], outputs[2])


def solution(mesh):
    return jax.shard_map(
        body,
        mesh=mesh,
        in_specs=(
            P(("blk", "head"), None),
            P(("blk", "head"), None),
            P(("blk", "head"), None),
            P(("blk", "head"), None),
            P(),
        ),
        out_specs=(P(("blk", "head"), None), P(("blk", "head"), None), P(("blk", "head"), None)),
        check_vma=False,
    )
```

profile of v0, /device:TPU:26, one launch (start us, length us, event | category | flops | bytes accessed | tf_op | source)
XLA Modules:
  0.0 104.3 jit_solution(3987964290970095193)
XLA Ops:
  0.7 1.2 %copy.101 = bf16[128,1024]{0,1:T(8,128)(2,1)S(1)} copy(bf16[128,1024]{1,0:T(8,128)(2,1)} %param.18) | data formatting | bytes 524288 | tf_op args[1]
  2.7 3.4 %all-to-all-start = ((bf16[128,4,256]{2,0,1:T(8,128)(2,1)}), bf16[128,4,256]{2,0,1:T(8,128)(2,1)S(1)}, u32[]{:S(2)}, u32[]{:S(2)}) async-start(bf16[128,4,256]{2,0,1:T(8,128)(2,1)} %copy.102), calls=%async_computation | async-start | bytes 524288 | tf_op jit(solution)/shard_map/all_to_all | solution.py:96
  9.4 2.7 %all-to-all-done = bf16[128,4,256]{2,0,1:T(8,128)(2,1)S(1)} async-done(((bf16[128,4,256]{2,0,1:T(8,128)(2,1)}), bf16[128,4,256]{2,0,1:T(8,128)(2,1)S(1)}, u32[]{:S(2)}, u32[]{:S(2)}) %all-to-all-start) | async-done | bytes 262176 | tf_op jit(solution)/shard_map/all_to_all | solution.py:96
  12.1 3.4 %all-to-all-start.1 = ((bf16[128,4,256]{2,0,1:T(8,128)(2,1)}), bf16[128,4,256]{2,0,1:T(8,128)(2,1)S(1)}, u32[]{:S(2)}, u32[]{:S(2)}) async-start(bf16[128,4,256]{2,0,1:T(8,128)(2,1)} %copy.104), calls=%async_computation.1 | async-start | bytes 524288 | tf_op jit(solution)/shard_map/all_to_all | solution.py:97
  16.3 5.2 %all-to-all-done.1 = bf16[128,4,256]{2,0,1:T(8,128)(2,1)S(1)} async-done(((bf16[128,4,256]{2,0,1:T(8,128)(2,1)}), bf16[128,4,256]{2,0,1:T(8,128)(2,1)S(1)}, u32[]{:S(2)}, u32[]{:S(2)}) %all-to-all-start.1) | async-done | bytes 262176 | tf_op jit(solution)/shard_map/all_to_all | solution.py:97
  21.5 3.4 %all-to-all-start.2 = ((bf16[128,4,256]{0,2,1:T(8,128)(2,1)}), bf16[128,4,256]{0,2,1:T(8,128)(2,1)S(1)}, u32[]{:S(2)}, u32[]{:S(2)}) async-start(bf16[128,4,256]{0,2,1:T(8,128)(2,1)} %bitcast.9), calls=%async_computation.2 | async-start | bytes 524288 | tf_op jit(solution)/shard_map/all_to_all | solution.py:95
  26.4 1.3 %collective-permute-start = (bf16[64,512]{0,1:T(8,128)(2,1)S(1)}, bf16[64,512]{0,1:T(8,128)(2,1)S(1)}, u32[]{:S(2)}, u32[]{:S(2)}) collective-permute-start(bf16[64,512]{0,1:T(8,128)(2,1)S(1)} %get-tuple-element.101), channel_id=1, source_target_pairs={{0,4},{4,8},{8,12},{12,16},{16,20},{20,24},{24,28},{1,5},{5,9},{9,... | collective-permute-start | bytes 196616 | tf_op jit(solution)/shard_map/ppermute | solution.py:15
  27.7 4.6 %collective-permute-start.1 = (bf16[64,512]{0,1:T(8,128)(2,1)S(1)}, bf16[64,512]{0,1:T(8,128)(2,1)S(1)}, u32[]{:S(2)}, u32[]{:S(2)}) collective-permute-start(bf16[64,512]{0,1:T(8,128)(2,1)S(1)} %get-tuple-element.102), channel_id=1, source_target_pairs={{4,0},{8,4},{12,8},{16,12},{20,16},{24,20},{28,24},{5,1},{9,5},{13... | collective-permute-start | bytes 196616 | tf_op jit(solution)/shard_map/ppermute | solution.py:18
  32.2 3.4 %all-to-all-start.3 = ((bf16[128,4,256]{0,2,1:T(8,128)(2,1)}), bf16[128,4,256]{0,2,1:T(8,128)(2,1)S(1)}, u32[]{:S(2)}, u32[]{:S(2)}) async-start(bf16[128,4,256]{0,2,1:T(8,128)(2,1)} %bitcast.14), calls=%async_computation.3 | async-start | bytes 524288 | tf_op jit(solution)/shard_map/all_to_all | solution.py:98
  35.7 6.0 %all-to-all-done.3 = bf16[128,4,256]{0,2,1:T(8,128)(2,1)S(1)} async-done(((bf16[128,4,256]{0,2,1:T(8,128)(2,1)}), bf16[128,4,256]{0,2,1:T(8,128)(2,1)S(1)}, u32[]{:S(2)}, u32[]{:S(2)}) %all-to-all-start.3) | async-done | bytes 262176 | tf_op jit(solution)/shard_map/all_to_all | solution.py:98
  43.0 0.9 convolution_convert_fusion.3
  45.4 0.9 convolution_convert_fusion.2
  46.4 1.0 fusion.45
  47.4 1.3 %fusion.64 = f32[4,256,64]{1,2,0:T(8,128)} fusion(bf16[128,4,64]{0,2,1:T(8,128)(2,1)S(1)} %bitcast.172, f32[4,128]{1,0:T(4,128)S(1)} %get-tuple-element.115, pred[128,256]{0,1:T(8,128)(4,1)S(1)} %fusion.84, bf16[256,4,64]{0,2,1:T(8,128)(2,1)S(1)} %bitcast.183, bf16[128,4,64]{0,2,1:T(8,128)(2,1)S(1)} %bitcast.197), kind=kOutput, calls=%fused_computation.78 | convolution fusion | flops 34341632 | bytes 559104 | tf_op jit(solution)/shard_map/hqk,qhd->khd/dot_general | solution.py:67
  48.9 1.2 %fusion.121 = (f32[4,128]{1,0:T(4,128)S(1)}, f32[4,128,256]{1,2,0:T(8,128)}) fusion(bf16[128,4,64]{0,2,1:T(8,128)(2,1)S(1)} %bitcast.191, bf16[256,4,64]{0,2,1:T(8,128)(2,1)S(1)} %bitcast.178, pred[128,256]{0,1:T(8,128)(4,1)S(1)} %copy-done.16), kind=kOutput, calls=%fused_computation.172 | convolution fusion | flops 17432832 | bytes 755712 | tf_op jit(solution)/shard_map/sub | solution.py:64
  51.4 1.3 %fusion.68 = f32[4,256,64]{1,2,0:T(8,128)} fusion(bf16[128,4,64]{0,2,1:T(8,128)(2,1)S(1)} %bitcast.168, f32[4,128]{1,0:T(4,128)S(1)} %get-tuple-element.119, pred[128,256]{0,1:T(8,128)(4,1)S(1)} %copy-done.15, bf16[128,4,64]{0,2,1:T(8,128)(2,1)S(1)} %bitcast.189, bf16[256,4,64]{0,2,1:T(8,128)(2,1)S(1)} %bitcast.176), kind=kOutput, calls=%fused_computation.82 | convolution fusion | flops 34341632 | bytes 559104 | tf_op jit(solution)/shard_map/hqk,qhd->khd/dot_general | solution.py:67
  52.7 1.5 %fusion.44 = f32[4,256,64]{1,2,0:T(8,128)S(1)} fusion(bf16[128,4,64]{0,2,1:T(8,128)(2,1)S(1)} %bitcast.193, f32[4,128,256]{1,2,0:T(8,128)S(1)} %fusion.125, f32[4,128,256]{1,2,0:T(8,128)} %get-tuple-element.118, f32[4,128]{1,0:T(4,128)S(1)} %get-tuple-element.117), kind=kOutput, calls=%fused_computation.56 | convolution fusion | flops 17695488 | bytes 1378304 | tf_op jit(solution)/shard_map/hqk,qhd->khd/dot_general | solution.py:78
  54.3 1.0 fusion.43
  55.4 0.9 copy-done.3
  57.6 1.3 %collective-permute-start.2 = (f32[64,512]{0,1:T(8,128)S(1)}, f32[64,512]{0,1:T(8,128)S(1)}, u32[]{:S(2)}, u32[]{:S(2)}) collective-permute-start(f32[64,512]{0,1:T(8,128)S(1)} %slice.255), channel_id=1, source_target_pairs={{0,4},{4,8},{8,12},{12,16},{16,20},{20,24},{24,28},{1,5},{5,9},{9,... | collective-permute-start | bytes 393224 | tf_op jit(solution)/shard_map/ppermute | solution.py:26
  59.0 1.5 %convolution_convert_fusion = bf16[4,128,64]{1,2,0:T(8,128)(2,1)S(1)} fusion(bf16[256,4,64]{0,2,1:T(8,128)(2,1)S(1)} %bitcast.180, f32[4,128,256]{1,2,0:T(8,128)S(1)} %fusion.125, f32[4,128,256]{1,2,0:T(8,128)} %get-tuple-element.118, f32[4,128]{1,0:T(4,128)S(1)} %get-tuple-element.117), kind=kOutput, calls=%fused_computation.50 | convolution fusion | flops 17728256 | bytes 1247232 | tf_op jit(solution)/shard_map/hqk,khd->qhd/dot_general | solution.py:75
  60.5 6.9 %collective-permute-done.2 = f32[64,512]{0,1:T(8,128)S(1)} collective-permute-done((f32[64,512]{0,1:T(8,128)S(1)}, f32[64,512]{0,1:T(8,128)S(1)}, u32[]{:S(2)}, u32[]{:S(2)}) %collective-permute-start.2) | collective-permute-done | bytes 131104 | tf_op jit(solution)/shard_map/ppermute | solution.py:26
  67.5 4.2 %collective-permute-start.3 = (f32[64,512]{0,1:T(8,128)S(1)}, f32[64,512]{0,1:T(8,128)S(1)}, u32[]{:S(2)}, u32[]{:S(2)}) collective-permute-start(f32[64,512]{0,1:T(8,128)S(1)} %get-tuple-element.91), channel_id=1, source_target_pairs={{4,0},{8,4},{12,8},{16,12},{20,16},{24,20},{28,24},{5,1},{9,5},{13... | collective-permute-start | bytes 393224 | tf_op jit(solution)/shard_map/ppermute | solution.py:26
  71.8 1.5 %convolution_convert_fusion.1 = bf16[4,128,64]{1,2,0:T(8,128)(2,1)S(1)} fusion(bf16[256,4,64]{0,2,1:T(8,128)(2,1)S(1)} %bitcast.177, f32[4,128,256]{1,2,0:T(8,128)S(1)} %fusion.124, f32[4,128,256]{1,2,0:T(8,128)} %copy-done.18, f32[4,128]{1,0:T(4,128)S(1)} %get-tuple-element.119), kind=kOutput, calls=%fused_computation.51 | convolution fusion | flops 17728256 | bytes 1247232 | tf_op jit(solution)/shard_map/hqk,khd->qhd/dot_general | solution.py:75
  75.0 3.4 %all-to-all-start.4 = ((bf16[4,128,256]{2,1,0:T(8,128)(2,1)}), bf16[4,128,256]{2,1,0:T(8,128)(2,1)S(1)}, u32[]{:S(2)}, u32[]{:S(2)}) async-start(bf16[4,128,256]{2,1,0:T(8,128)(2,1)} %bitcast.42), calls=%async_computation.4 | async-start | bytes 524288 | tf_op jit(solution)/shard_map/all_to_all | solution.py:113
  78.5 1.9 %scatter-add.26 = f32[512,512]{0,1:T(8,128)S(1)} dynamic-update-slice(f32[512,512]{0,1:T(8,128)S(1)} %slice.253, f32[64,512]{0,1:T(8,128)S(1)} %get-tuple-element.92, s32[]{:T(128)} %constant.187.clone.1, s32[]{:T(128)} %constant.187.clone.1) | dynamic-update-slice | bytes 262148 | tf_op jit(solution)/shard_map/scatter-add | solution.py:111
  80.5 1.5 %scatter-add.29 = f32[512,512]{0,1:T(8,128)S(1)} dynamic-update-slice(f32[512,512]{0,1:T(8,128)S(1)} %scatter-add.26, f32[64,512]{0,1:T(8,128)S(1)} %slice_add_fusion.3, s32[]{:T(128)} %constant.198.clone.1, s32[]{:T(128)} %constant.187.clone.1) | dynamic-update-slice | bytes 262148 | tf_op jit(solution)/shard_map/scatter-add | solution.py:111
  83.0 1.5 %all-to-all-done.4 = bf16[4,128,256]{2,1,0:T(8,128)(2,1)S(1)} async-done(((bf16[4,128,256]{2,1,0:T(8,128)(2,1)}), bf16[4,128,256]{2,1,0:T(8,128)(2,1)S(1)}, u32[]{:S(2)}, u32[]{:S(2)}) %all-to-all-start.4) | async-done | bytes 262176 | tf_op jit(solution)/shard_map/all_to_all | solution.py:113
  84.5 3.4 %all-to-all-start.6 = ((bf16[4,128,256]{2,1,0:T(8,128)(2,1)}), bf16[4,128,256]{2,1,0:T(8,128)(2,1)S(1)}, u32[]{:S(2)}, u32[]{:S(2)}) async-start(bf16[4,128,256]{2,1,0:T(8,128)(2,1)} %bitcast.64), calls=%async_computation.6 | async-start | bytes 524288 | tf_op jit(solution)/shard_map/all_to_all | solution.py:123
  88.7 5.2 %all-to-all-done.6 = bf16[4,128,256]{2,1,0:T(8,128)(2,1)S(1)} async-done(((bf16[4,128,256]{2,1,0:T(8,128)(2,1)}), bf16[4,128,256]{2,1,0:T(8,128)(2,1)S(1)}, u32[]{:S(2)}, u32[]{:S(2)}) %all-to-all-start.6) | async-done | bytes 262176 | tf_op jit(solution)/shard_map/all_to_all | solution.py:123
  93.9 3.4 %all-to-all-start.5 = ((bf16[4,128,256]{2,1,0:T(8,128)(2,1)}), bf16[4,128,256]{2,1,0:T(8,128)(2,1)S(1)}, u32[]{:S(2)}, u32[]{:S(2)}) async-start(bf16[4,128,256]{2,1,0:T(8,128)(2,1)} %bitcast.61), calls=%async_computation.5 | async-start | bytes 524288 | tf_op jit(solution)/shard_map/all_to_all | solution.py:116
  99.4 3.9 %all-to-all-done.5 = bf16[4,128,256]{2,1,0:T(8,128)(2,1)S(1)} async-done(((bf16[4,128,256]{2,1,0:T(8,128)(2,1)}), bf16[4,128,256]{2,1,0:T(8,128)(2,1)S(1)}, u32[]{:S(2)}, u32[]{:S(2)}) %all-to-all-start.5) | async-done | bytes 262176 | tf_op jit(solution)/shard_map/all_to_all | solution.py:116
  (95 shorter events, 19.0 us)
Async XLA Ops:
  0.6 5.6 %copy-start = (bf16[128,1024]{1,0:T(8,128)(2,1)S(1)}, bf16[128,1024]{1,0:T(8,128)(2,1)}, u32[]{:S(2)}) copy-start(bf16[128,1024]{1,0:T(8,128)(2,1)} %param.17) | copy-start | bytes 786436
  0.6 6.4 %copy-start.1 = (bf16[128,1024]{1,0:T(8,128)(2,1)S(1)}, bf16[128,1024]{1,0:T(8,128)(2,1)}, u32[]{:S(2)}) copy-start(bf16[128,1024]{1,0:T(8,128)(2,1)} %param.19) | copy-start | bytes 786436
  1.8 6.3 %copy-start.17 = (s32[4]{0:T(128)S(1)}, s32[4]{0:T(128)}, u32[]{:S(2)}) copy-start(s32[4]{0:T(128)} %param.21) | copy-start | bytes 52
  2.7 9.4 %all-to-all-start = ((bf16[128,4,256]{2,0,1:T(8,128)(2,1)}), bf16[128,4,256]{2,0,1:T(8,128)(2,1)S(1)}, u32[]{:S(2)}, u32[]{:S(2)}) async-start(bf16[128,4,256]{2,0,1:T(8,128)(2,1)} %copy.102), calls=%async_computation | async-start | bytes 524288 | tf_op jit(solution)/shard_map/all_to_all | solution.py:96
  6.2 18.9 %copy-start.2 = (bf16[128,1024]{1,0:T(8,128)(2,1)S(1)}, bf16[128,1024]{1,0:T(8,128)(2,1)}, u32[]{:S(2)}) copy-start(bf16[128,1024]{1,0:T(8,128)(2,1)} %param.20) | copy-start | bytes 786436
  12.1 9.4 %all-to-all-start.1 = ((bf16[128,4,256]{2,0,1:T(8,128)(2,1)}), bf16[128,4,256]{2,0,1:T(8,128)(2,1)S(1)}, u32[]{:S(2)}, u32[]{:S(2)}) async-start(bf16[128,4,256]{2,0,1:T(8,128)(2,1)} %copy.104), calls=%async_computation.1 | async-start | bytes 524288 | tf_op jit(solution)/shard_map/all_to_all | solution.py:97
  21.5 10.7 %all-to-all-start.2 = ((bf16[128,4,256]{0,2,1:T(8,128)(2,1)}), bf16[128,4,256]{0,2,1:T(8,128)(2,1)S(1)}, u32[]{:S(2)}, u32[]{:S(2)}) async-start(bf16[128,4,256]{0,2,1:T(8,128)(2,1)} %bitcast.9), calls=%async_computation.2 | async-start | bytes 524288 | tf_op jit(solution)/shard_map/all_to_all | solution.py:95
  26.4 15.3 %collective-permute-start = (bf16[64,512]{0,1:T(8,128)(2,1)S(1)}, bf16[64,512]{0,1:T(8,128)(2,1)S(1)}, u32[]{:S(2)}, u32[]{:S(2)}) collective-permute-start(bf16[64,512]{0,1:T(8,128)(2,1)S(1)} %get-tuple-element.101), channel_id=1, source_target_pairs={{0,4},{4,8},{8,12},{12,16},{16,20},{20,24},{24,28},{1,5},{5,9},{9,... | collective-permute-start | bytes 196616 | tf_op jit(solution)/shard_map/ppermute | solution.py:15
  27.7 14.0 %collective-permute-start.1 = (bf16[64,512]{0,1:T(8,128)(2,1)S(1)}, bf16[64,512]{0,1:T(8,128)(2,1)S(1)}, u32[]{:S(2)}, u32[]{:S(2)}) collective-permute-start(bf16[64,512]{0,1:T(8,128)(2,1)S(1)} %get-tuple-element.102), channel_id=1, source_target_pairs={{4,0},{8,4},{12,8},{16,12},{20,16},{24,20},{28,24},{5,1},{9,5},{13... | collective-permute-start | bytes 196616 | tf_op jit(solution)/shard_map/ppermute | solution.py:18
  32.2 9.4 %all-to-all-start.3 = ((bf16[128,4,256]{0,2,1:T(8,128)(2,1)}), bf16[128,4,256]{0,2,1:T(8,128)(2,1)S(1)}, u32[]{:S(2)}, u32[]{:S(2)}) async-start(bf16[128,4,256]{0,2,1:T(8,128)(2,1)} %bitcast.14), calls=%async_computation.3 | async-start | bytes 524288 | tf_op jit(solution)/shard_map/all_to_all | solution.py:98
  35.7 14.4 %copy-start.12 = (bf16[1,128,256]{1,2,0:T(8,128)(2,1)}, bf16[1,128,256]{1,2,0:T(8,128)(2,1)S(1)}, u32[]{:S(2)}) copy-start(bf16[1,128,256]{1,2,0:T(8,128)(2,1)S(1)} %get-tuple-element.105) | copy-start | bytes 196612
  35.7 15.7 %copy-start.10 = (bf16[1,128,256]{1,2,0:T(8,128)(2,1)}, bf16[1,128,256]{1,2,0:T(8,128)(2,1)S(1)}, u32[]{:S(2)}) copy-start(bf16[1,128,256]{1,2,0:T(8,128)(2,1)S(1)} %get-tuple-element.106) | copy-start | bytes 196612
  42.3 7.9 %copy-start.7 = (bf16[256,256]{0,1:T(8,128)(2,1)}, bf16[256,256]{0,1:T(8,128)(2,1)S(1)}, u32[]{:S(2)}) copy-start(bf16[256,256]{0,1:T(8,128)(2,1)S(1)} %get-tuple-element.111) | copy-start | bytes 393220
  47.4 1.6 %copy-start.16 = (pred[128,256]{0,1:T(8,128)(4,1)S(1)}, pred[128,256]{0,1:T(8,128)(4,1)}, u32[]{:S(2)}) copy-start(pred[128,256]{0,1:T(8,128)(4,1)} %fusion.85) | copy-start | bytes 98308
  50.1 0.9 copy-start.15
  51.4 2.8 %copy-start.18 = (f32[4,128,256]{1,2,0:T(8,128)}, f32[4,128,256]{1,2,0:T(8,128)S(1)}, u32[]{:S(2)}) copy-start(f32[4,128,256]{1,2,0:T(8,128)S(1)} %get-tuple-element.120) | copy-start | bytes 1572868
  51.4 1.3 %copy-start.13 = (bf16[1,128,256]{1,2,0:T(8,128)(2,1)S(1)}, bf16[1,128,256]{1,2,0:T(8,128)(2,1)}, u32[]{:S(2)}) copy-start(bf16[1,128,256]{1,2,0:T(8,128)(2,1)} %copy-done.12) | copy-start | bytes 196612
  52.7 1.6 %copy-start.11 = (bf16[1,128,256]{1,2,0:T(8,128)(2,1)S(1)}, bf16[1,128,256]{1,2,0:T(8,128)(2,1)}, u32[]{:S(2)}) copy-start(bf16[1,128,256]{1,2,0:T(8,128)(2,1)} %copy-done.10) | copy-start | bytes 196612
  55.3 0.9 copy-start.3
  55.3 1.0 copy-start.4
  56.3 0.9 copy-start.5
  56.3 1.0 copy-start.6
  57.3 1.6 %copy-start.8 = (bf16[256,256]{0,1:T(8,128)(2,1)S(1)}, bf16[256,256]{0,1:T(8,128)(2,1)}, u32[]{:S(2)}) copy-start(bf16[256,256]{0,1:T(8,128)(2,1)} %copy-done.7) | copy-start | bytes 393220
  57.6 9.7 %collective-permute-start.2 = (f32[64,512]{0,1:T(8,128)S(1)}, f32[64,512]{0,1:T(8,128)S(1)}, u32[]{:S(2)}, u32[]{:S(2)}) collective-permute-start(f32[64,512]{0,1:T(8,128)S(1)} %slice.255), channel_id=1, source_target_pairs={{0,4},{4,8},{8,12},{12,16},{16,20},{20,24},{24,28},{1,5},{5,9},{9,... | collective-permute-start | bytes 393224 | tf_op jit(solution)/shard_map/ppermute | solution.py:26
  67.5 12.9 %collective-permute-start.3 = (f32[64,512]{0,1:T(8,128)S(1)}, f32[64,512]{0,1:T(8,128)S(1)}, u32[]{:S(2)}, u32[]{:S(2)}) collective-permute-start(f32[64,512]{0,1:T(8,128)S(1)} %get-tuple-element.91), channel_id=1, source_target_pairs={{4,0},{8,4},{12,8},{16,12},{20,16},{24,20},{28,24},{5,1},{9,5},{13... | collective-permute-start | bytes 393224 | tf_op jit(solution)/shard_map/ppermute | solution.py:26
  73.3 0.8 copy-start.9
  73.3 0.9 copy-start.14
  75.0 9.4 %all-to-all-start.4 = ((bf16[4,128,256]{2,1,0:T(8,128)(2,1)}), bf16[4,128,256]{2,1,0:T(8,128)(2,1)S(1)}, u32[]{:S(2)}, u32[]{:S(2)}) async-start(bf16[4,128,256]{2,1,0:T(8,128)(2,1)} %bitcast.42), calls=%async_computation.4 | async-start | bytes 524288 | tf_op jit(solution)/shard_map/all_to_all | solution.py:113
  84.5 9.4 %all-to-all-start.6 = ((bf16[4,128,256]{2,1,0:T(8,128)(2,1)}), bf16[4,128,256]{2,1,0:T(8,128)(2,1)S(1)}, u32[]{:S(2)}, u32[]{:S(2)}) async-start(bf16[4,128,256]{2,1,0:T(8,128)(2,1)} %bitcast.64), calls=%async_computation.6 | async-start | bytes 524288 | tf_op jit(solution)/shard_map/all_to_all | solution.py:123
  93.9 9.4 %all-to-all-start.5 = ((bf16[4,128,256]{2,1,0:T(8,128)(2,1)}), bf16[4,128,256]{2,1,0:T(8,128)(2,1)S(1)}, u32[]{:S(2)}, u32[]{:S(2)}) async-start(bf16[4,128,256]{2,1,0:T(8,128)(2,1)} %bitcast.61), calls=%async_computation.5 | async-start | bytes 524288 | tf_op jit(solution)/shard_map/all_to_all | solution.py:116
where the time goes:
time: 105 us; the launch traced here: 104 us
  starting transfers between devices  35.2 us (34%)
  waiting for transfers between devices  31.4 us (30%)
  local copies, waits for them, and re-layouts  16.8 us (16%)
  matrix products  15.9 us (15%)
  other arithmetic  3.8 us (4%)
  between operations  1.16 us (1%)
    ppermute x2, waiting for transfers between devices, shifted(): return lax.ppermute(block, axis, route)  6.94 us
    unnamed x43, local copies, waits for them, and re-layouts  6.22 us
    all_to_all x1, waiting for transfers between devices, body(): lax.all_to_all(grad_output, 'head', split_axis=1, concat_axis=0, tiled=True)  5.95 us
    ppermute x2, starting transfers between devices, shifted(): return lax.ppermute(block, axis, route)  5.54 us
    all_to_all x1, waiting for transfers between devices, body(): lax.all_to_all(value_vectors, 'head', split_axis=1, concat_axis=0, tiled=...  5.22 us
    all_to_all x1, waiting for transfers between devices, body(): lax.all_to_all(own_rows[:, columns:].astype(jnp.bfloat16), 'head', split_...  5.16 us
    dot_general x4, matrix products, band_grads(): jnp.einsum('hqk,khd->qhd', score_grad, key_block, preferred_element_type=...  4.84 us
    ppermute x1, starting transfers between devices, with_halo(): lax.ppermute(lax.slice_in_dim(block, 0, width, axis=dim), axis, backward)  4.55 us
  transfers between devices with their start and end apart: 11, of which 7 were waited for; matrix products, arithmetic and copies ran while one was open for 16% of the time, Pallas kernels for 0%

commit v1 on v0

--- a/solution.py
+++ b/solution.py
@@ -120,12 +120,18 @@
             concat_axis=1,
             tiled=True,
         ),
-        lax.all_to_all(
-            own_rows[:, columns:].astype(jnp.bfloat16),
-            "head",
-            split_axis=0,
-            concat_axis=1,
-            tiled=True,
+        jnp.concatenate(
+            lax.all_to_all(
+                jnp.stack(
+                    jnp.split(
+                        own_rows[:, columns:].astype(jnp.bfloat16), lax.axis_size("head"), axis=0
+                    )
+                ),
+                "head",
+                0,
+                0,
+            ),
+            axis=1,
         ),
     )
     return (outputs[0], outputs[1], outputs[2])

time: 105 us -> 105 us (level)
    all_to_all x1, waiting for transfers between devices: 3.94 us -> 5.21 us  [body(): lax.all_to_all(own_rows[:, :columns].astype(jnp.bfloat16), 'head', split_...]
    all_to_all x1, waiting for transfers between devices: 5.16 us -> 3.94 us  [body(): lax.all_to_all(jnp.stack(jnp.split(own_rows[:, columns:].astype(jnp.bfloa...]
    unnamed x43 -> x42, local copies, waits for them, and re-layouts: 6.22 us -> 5.37 us
where the time goes in v1:
time: 105 us; the launch traced here: 104 us
  starting transfers between devices  35.2 us (34%)
  waiting for transfers between devices  31.5 us (30%)
  matrix products  15.9 us (15%)
  local copies, waits for them, and re-layouts  15.8 us (15%)
  other arithmetic  4.53 us (4%)
  between operations  1.16 us (1%)
    ppermute x2, waiting for transfers between devices, shifted(): return lax.ppermute(block, axis, route)  6.94 us
    all_to_all x1, waiting for transfers between devices, body(): lax.all_to_all(grad_output, 'head', split_axis=1, concat_axis=0, tiled=True)  5.95 us
    ppermute x2, starting transfers between devices, shifted(): return lax.ppermute(block, axis, route)  5.54 us
    unnamed x42, local copies, waits for them, and re-layouts  5.37 us
    all_to_all x1, waiting for transfers between devices, body(): lax.all_to_all(value_vectors, 'head', split_axis=1, concat_axis=0, tiled=...  5.22 us
    all_to_all x1, waiting for transfers between devices, body(): lax.all_to_all(own_rows[:, :columns].astype(jnp.bfloat16), 'head', split_...  5.21 us
    dot_general x4, matrix products, band_grads(): jnp.einsum('hqk,khd->qhd', score_grad, key_block, preferred_element_type=...  4.84 us
    ppermute x1, starting transfers between devices, with_halo(): lax.ppermute(lax.slice_in_dim(block, 0, width, axis=dim), axis, backward)  4.55 us
  transfers between devices with their start and end apart: 11, of which 7 were waited for; matrix products, arithmetic and copies ran while one was open for 16% of the time, Pallas kernels for 0%

profile of v1, /device:TPU:26, one launch (start us, length us, event | category | flops | bytes accessed | tf_op | source)
XLA Modules:
  0.0 104.2 jit_solution(11933426857336777404)
XLA Ops:
  0.7 1.2 %copy.99 = bf16[128,1024]{0,1:T(8,128)(2,1)S(1)} copy(bf16[128,1024]{1,0:T(8,128)(2,1)} %param.18) | data formatting | bytes 524288 | tf_op args[1]
  2.7 3.4 %all-to-all-start = ((bf16[128,4,256]{2,0,1:T(8,128)(2,1)}), bf16[128,4,256]{2,0,1:T(8,128)(2,1)S(1)}, u32[]{:S(2)}, u32[]{:S(2)}) async-start(bf16[128,4,256]{2,0,1:T(8,128)(2,1)} %copy.100), calls=%async_computation | async-start | bytes 524288 | tf_op jit(solution)/shard_map/all_to_all | solution.py:96
  9.4 2.7 %all-to-all-done = bf16[128,4,256]{2,0,1:T(8,128)(2,1)S(1)} async-done(((bf16[128,4,256]{2,0,1:T(8,128)(2,1)}), bf16[128,4,256]{2,0,1:T(8,128)(2,1)S(1)}, u32[]{:S(2)}, u32[]{:S(2)}) %all-to-all-start) | async-done | bytes 262176 | tf_op jit(solution)/shard_map/all_to_all | solution.py:96
  12.1 3.4 %all-to-all-start.1 = ((bf16[128,4,256]{2,0,1:T(8,128)(2,1)}), bf16[128,4,256]{2,0,1:T(8,128)(2,1)S(1)}, u32[]{:S(2)}, u32[]{:S(2)}) async-start(bf16[128,4,256]{2,0,1:T(8,128)(2,1)} %copy.102), calls=%async_computation.1 | async-start | bytes 524288 | tf_op jit(solution)/shard_map/all_to_all | solution.py:97
  16.3 5.2 %all-to-all-done.1 = bf16[128,4,256]{2,0,1:T(8,128)(2,1)S(1)} async-done(((bf16[128,4,256]{2,0,1:T(8,128)(2,1)}), bf16[128,4,256]{2,0,1:T(8,128)(2,1)S(1)}, u32[]{:S(2)}, u32[]{:S(2)}) %all-to-all-start.1) | async-done | bytes 262176 | tf_op jit(solution)/shard_map/all_to_all | solution.py:97
  21.5 3.4 %all-to-all-start.2 = ((bf16[128,4,256]{0,2,1:T(8,128)(2,1)}), bf16[128,4,256]{0,2,1:T(8,128)(2,1)S(1)}, u32[]{:S(2)}, u32[]{:S(2)}) async-start(bf16[128,4,256]{0,2,1:T(8,128)(2,1)} %bitcast.9), calls=%async_computation.2 | async-start | bytes 524288 | tf_op jit(solution)/shard_map/all_to_all | solution.py:95
  26.4 1.3 %collective-permute-start = (bf16[64,512]{0,1:T(8,128)(2,1)S(1)}, bf16[64,512]{0,1:T(8,128)(2,1)S(1)}, u32[]{:S(2)}, u32[]{:S(2)}) collective-permute-start(bf16[64,512]{0,1:T(8,128)(2,1)S(1)} %get-tuple-element.103), channel_id=1, source_target_pairs={{0,4},{4,8},{8,12},{12,16},{16,20},{20,24},{24,28},{1,5},{5,9},{9,... | collective-permute-start | bytes 196616 | tf_op jit(solution)/shard_map/ppermute | solution.py:15
  27.7 4.6 %collective-permute-start.1 = (bf16[64,512]{0,1:T(8,128)(2,1)S(1)}, bf16[64,512]{0,1:T(8,128)(2,1)S(1)}, u32[]{:S(2)}, u32[]{:S(2)}) collective-permute-start(bf16[64,512]{0,1:T(8,128)(2,1)S(1)} %get-tuple-element.104), channel_id=1, source_target_pairs={{4,0},{8,4},{12,8},{16,12},{20,16},{24,20},{28,24},{5,1},{9,5},{13... | collective-permute-start | bytes 196616 | tf_op jit(solution)/shard_map/ppermute | solution.py:18
  32.2 3.4 %all-to-all-start.3 = ((bf16[128,4,256]{0,2,1:T(8,128)(2,1)}), bf16[128,4,256]{0,2,1:T(8,128)(2,1)S(1)}, u32[]{:S(2)}, u32[]{:S(2)}) async-start(bf16[128,4,256]{0,2,1:T(8,128)(2,1)} %bitcast.14), calls=%async_computation.3 | async-start | bytes 524288 | tf_op jit(solution)/shard_map/all_to_all | solution.py:98
  35.7 6.0 %all-to-all-done.3 = bf16[128,4,256]{0,2,1:T(8,128)(2,1)S(1)} async-done(((bf16[128,4,256]{0,2,1:T(8,128)(2,1)}), bf16[128,4,256]{0,2,1:T(8,128)(2,1)S(1)}, u32[]{:S(2)}, u32[]{:S(2)}) %all-to-all-start.3) | async-done | bytes 262176 | tf_op jit(solution)/shard_map/all_to_all | solution.py:98
  43.0 0.9 convolution_convert_fusion.3
  45.4 0.9 convolution_convert_fusion.2
  46.4 1.0 fusion.45
  47.4 1.3 %fusion.64 = f32[4,256,64]{1,2,0:T(8,128)} fusion(bf16[128,4,64]{0,2,1:T(8,128)(2,1)S(1)} %bitcast.179, f32[4,128]{1,0:T(4,128)S(1)} %get-tuple-element.117, pred[128,256]{0,1:T(8,128)(4,1)S(1)} %fusion.84, bf16[256,4,64]{0,2,1:T(8,128)(2,1)S(1)} %bitcast.190, bf16[128,4,64]{0,2,1:T(8,128)(2,1)S(1)} %bitcast.204), kind=kOutput, calls=%fused_computation.79 | convolution fusion | flops 34341632 | bytes 559104 | tf_op jit(solution)/shard_map/hqk,qhd->khd/dot_general | solution.py:67
  48.9 1.2 %fusion.120 = (f32[4,128]{1,0:T(4,128)S(1)}, f32[4,128,256]{1,2,0:T(8,128)}) fusion(bf16[128,4,64]{0,2,1:T(8,128)(2,1)S(1)} %bitcast.198, bf16[256,4,64]{0,2,1:T(8,128)(2,1)S(1)} %bitcast.185, pred[128,256]{0,1:T(8,128)(4,1)S(1)} %copy-done.16), kind=kOutput, calls=%fused_computation.176 | convolution fusion | flops 17432832 | bytes 755712 | tf_op jit(solution)/shard_map/sub | solution.py:64
  51.4 1.3 %fusion.68 = f32[4,256,64]{1,2,0:T(8,128)} fusion(bf16[128,4,64]{0,2,1:T(8,128)(2,1)S(1)} %bitcast.175, f32[4,128]{1,0:T(4,128)S(1)} %get-tuple-element.121, pred[128,256]{0,1:T(8,128)(4,1)S(1)} %copy-done.15, bf16[128,4,64]{0,2,1:T(8,128)(2,1)S(1)} %bitcast.196, bf16[256,4,64]{0,2,1:T(8,128)(2,1)S(1)} %bitcast.183), kind=kOutput, calls=%fused_computation.83 | convolution fusion | flops 34341632 | bytes 559104 | tf_op jit(solution)/shard_map/hqk,qhd->khd/dot_general | solution.py:67
  52.7 1.5 %fusion.44 = f32[4,256,64]{1,2,0:T(8,128)S(1)} fusion(bf16[128,4,64]{0,2,1:T(8,128)(2,1)S(1)} %bitcast.200, f32[4,128,256]{1,2,0:T(8,128)S(1)} %fusion.124, f32[4,128,256]{1,2,0:T(8,128)} %get-tuple-element.120, f32[4,128]{1,0:T(4,128)S(1)} %get-tuple-element.119), kind=kOutput, calls=%fused_computation.56 | convolution fusion | flops 17695488 | bytes 1378304 | tf_op jit(solution)/shard_map/hqk,qhd->khd/dot_general | solution.py:78
  54.3 1.0 fusion.43
  55.4 0.9 copy-done.3
  57.6 1.3 %collective-permute-start.2 = (f32[64,512]{0,1:T(8,128)S(1)}, f32[64,512]{0,1:T(8,128)S(1)}, u32[]{:S(2)}, u32[]{:S(2)}) collective-permute-start(f32[64,512]{0,1:T(8,128)S(1)} %slice.256), channel_id=1, source_target_pairs={{0,4},{4,8},{8,12},{12,16},{16,20},{20,24},{24,28},{1,5},{5,9},{9,... | collective-permute-start | bytes 393224 | tf_op jit(solution)/shard_map/ppermute | solution.py:26
  59.0 1.5 %convolution_convert_fusion = bf16[4,128,64]{1,2,0:T(8,128)(2,1)S(1)} fusion(bf16[256,4,64]{0,2,1:T(8,128)(2,1)S(1)} %bitcast.187, f32[4,128,256]{1,2,0:T(8,128)S(1)} %fusion.124, f32[4,128,256]{1,2,0:T(8,128)} %get-tuple-element.120, f32[4,128]{1,0:T(4,128)S(1)} %get-tuple-element.119), kind=kOutput, calls=%fused_computation.50 | convolution fusion | flops 17728256 | bytes 1247232 | tf_op jit(solution)/shard_map/hqk,khd->qhd/dot_general | solution.py:75
  60.5 6.9 %collective-permute-done.2 = f32[64,512]{0,1:T(8,128)S(1)} collective-permute-done((f32[64,512]{0,1:T(8,128)S(1)}, f32[64,512]{0,1:T(8,128)S(1)}, u32[]{:S(2)}, u32[]{:S(2)}) %collective-permute-start.2) | collective-permute-done | bytes 131104 | tf_op jit(solution)/shard_map/ppermute | solution.py:26
  67.5 4.2 %collective-permute-start.3 = (f32[64,512]{0,1:T(8,128)S(1)}, f32[64,512]{0,1:T(8,128)S(1)}, u32[]{:S(2)}, u32[]{:S(2)}) collective-permute-start(f32[64,512]{0,1:T(8,128)S(1)} %get-tuple-element.91), channel_id=1, source_target_pairs={{4,0},{8,4},{12,8},{16,12},{20,16},{24,20},{28,24},{5,1},{9,5},{13... | collective-permute-start | bytes 393224 | tf_op jit(solution)/shard_map/ppermute | solution.py:26
  71.8 1.5 %convolution_convert_fusion.1 = bf16[4,128,64]{1,2,0:T(8,128)(2,1)S(1)} fusion(bf16[256,4,64]{0,2,1:T(8,128)(2,1)S(1)} %bitcast.184, f32[4,128,256]{1,2,0:T(8,128)S(1)} %fusion.123, f32[4,128,256]{1,2,0:T(8,128)} %copy-done.18, f32[4,128]{1,0:T(4,128)S(1)} %get-tuple-element.121), kind=kOutput, calls=%fused_computation.51 | convolution fusion | flops 17728256 | bytes 1247232 | tf_op jit(solution)/shard_map/hqk,khd->qhd/dot_general | solution.py:75
  75.0 3.4 %all-to-all-start.4 = ((bf16[4,128,256]{2,1,0:T(8,128)(2,1)}), bf16[4,128,256]{2,1,0:T(8,128)(2,1)S(1)}, u32[]{:S(2)}, u32[]{:S(2)}) async-start(bf16[4,128,256]{2,1,0:T(8,128)(2,1)} %bitcast.42), calls=%async_computation.4 | async-start | bytes 524288 | tf_op jit(solution)/shard_map/all_to_all | solution.py:113
  78.5 1.9 %scatter-add.26 = f32[512,512]{0,1:T(8,128)S(1)} dynamic-update-slice(f32[512,512]{0,1:T(8,128)S(1)} %slice.254, f32[64,512]{0,1:T(8,128)S(1)} %get-tuple-element.92, s32[]{:T(128)} %constant.187.clone.1, s32[]{:T(128)} %constant.187.clone.1) | dynamic-update-slice | bytes 262148 | tf_op jit(solution)/shard_map/scatter-add | solution.py:111
  80.5 1.5 %scatter-add.29 = f32[512,512]{0,1:T(8,128)S(1)} dynamic-update-slice(f32[512,512]{0,1:T(8,128)S(1)} %scatter-add.26, f32[64,512]{0,1:T(8,128)S(1)} %slice_add_fusion.3, s32[]{:T(128)} %constant.198.clone.1, s32[]{:T(128)} %constant.187.clone.1) | dynamic-update-slice | bytes 262148 | tf_op jit(solution)/shard_map/scatter-add | solution.py:111
  83.0 1.5 %all-to-all-done.4 = bf16[4,128,256]{2,1,0:T(8,128)(2,1)S(1)} async-done(((bf16[4,128,256]{2,1,0:T(8,128)(2,1)}), bf16[4,128,256]{2,1,0:T(8,128)(2,1)S(1)}, u32[]{:S(2)}, u32[]{:S(2)}) %all-to-all-start.4) | async-done | bytes 262176 | tf_op jit(solution)/shard_map/all_to_all | solution.py:113
  84.5 3.4 %all-to-all-start.5 = ((bf16[4,128,256]{2,1,0:T(8,128)(2,1)}), bf16[4,128,256]{2,1,0:T(8,128)(2,1)S(1)}, u32[]{:S(2)}, u32[]{:S(2)}) async-start(bf16[4,128,256]{2,1,0:T(8,128)(2,1)} %bitcast.61), calls=%async_computation.5 | async-start | bytes 524288 | tf_op jit(solution)/shard_map/all_to_all | solution.py:116
  88.7 5.2 %all-to-all-done.5 = bf16[4,128,256]{2,1,0:T(8,128)(2,1)S(1)} async-done(((bf16[4,128,256]{2,1,0:T(8,128)(2,1)}), bf16[4,128,256]{2,1,0:T(8,128)(2,1)S(1)}, u32[]{:S(2)}, u32[]{:S(2)}) %all-to-all-start.5) | async-done | bytes 262176 | tf_op jit(solution)/shard_map/all_to_all | solution.py:116
  93.9 3.4 %all-to-all-start.6 = ((bf16[4,128,256]{1,2,0:T(8,128)(2,1)}), bf16[4,128,256]{1,2,0:T(8,128)(2,1)S(1)}, u32[]{:S(2)}, u32[]{:S(2)}) async-start(bf16[4,128,256]{1,2,0:T(8,128)(2,1)} %pad_maximum_fusion.1), calls=%async_computation.6 | async-start | bytes 524288 | tf_op jit(solution)/shard_map/all_to_all | solution.py:124
  99.4 3.9 %all-to-all-done.6 = bf16[4,128,256]{1,2,0:T(8,128)(2,1)S(1)} async-done(((bf16[4,128,256]{1,2,0:T(8,128)(2,1)}), bf16[4,128,256]{1,2,0:T(8,128)(2,1)S(1)}, u32[]{:S(2)}, u32[]{:S(2)}) %all-to-all-start.6) | async-done | bytes 262176 | tf_op jit(solution)/shard_map/all_to_all | solution.py:124
  (95 shorter events, 18.7 us)
Async XLA Ops:
  0.6 5.6 %copy-start = (bf16[128,1024]{1,0:T(8,128)(2,1)S(1)}, bf16[128,1024]{1,0:T(8,128)(2,1)}, u32[]{:S(2)}) copy-start(bf16[128,1024]{1,0:T(8,128)(2,1)} %param.17) | copy-start | bytes 786436
  0.6 6.4 %copy-start.1 = (bf16[128,1024]{1,0:T(8,128)(2,1)S(1)}, bf16[128,1024]{1,0:T(8,128)(2,1)}, u32[]{:S(2)}) copy-start(bf16[128,1024]{1,0:T(8,128)(2,1)} %param.19) | copy-start | bytes 786436
  1.8 6.3 %copy-start.17 = (s32[4]{0:T(128)S(1)}, s32[4]{0:T(128)}, u32[]{:S(2)}) copy-start(s32[4]{0:T(128)} %param.21) | copy-start | bytes 52
  2.7 9.4 %all-to-all-start = ((bf16[128,4,256]{2,0,1:T(8,128)(2,1)}), bf16[128,4,256]{2,0,1:T(8,128)(2,1)S(1)}, u32[]{:S(2)}, u32[]{:S(2)}) async-start(bf16[128,4,256]{2,0,1:T(8,128)(2,1)} %copy.100), calls=%async_computation | async-start | bytes 524288 | tf_op jit(solution)/shard_map/all_to_all | solution.py:96
  6.2 18.9 %copy-start.2 = (bf16[128,1024]{1,0:T(8,128)(2,1)S(1)}, bf16[128,1024]{1,0:T(8,128)(2,1)}, u32[]{:S(2)}) copy-start(bf16[128,1024]{1,0:T(8,128)(2,1)} %param.20) | copy-start | bytes 786436
  12.1 9.4 %all-to-all-start.1 = ((bf16[128,4,256]{2,0,1:T(8,128)(2,1)}), bf16[128,4,256]{2,0,1:T(8,128)(2,1)S(1)}, u32[]{:S(2)}, u32[]{:S(2)}) async-start(bf16[128,4,256]{2,0,1:T(8,128)(2,1)} %copy.102), calls=%async_computation.1 | async-start | bytes 524288 | tf_op jit(solution)/shard_map/all_to_all | solution.py:97
  21.5 10.7 %all-to-all-start.2 = ((bf16[128,4,256]{0,2,1:T(8,128)(2,1)}), bf16[128,4,256]{0,2,1:T(8,128)(2,1)S(1)}, u32[]{:S(2)}, u32[]{:S(2)}) async-start(bf16[128,4,256]{0,2,1:T(8,128)(2,1)} %bitcast.9), calls=%async_computation.2 | async-start | bytes 524288 | tf_op jit(solution)/shard_map/all_to_all | solution.py:95
  26.4 15.3 %collective-permute-start = (bf16[64,512]{0,1:T(8,128)(2,1)S(1)}, bf16[64,512]{0,1:T(8,128)(2,1)S(1)}, u32[]{:S(2)}, u32[]{:S(2)}) collective-permute-start(bf16[64,512]{0,1:T(8,128)(2,1)S(1)} %get-tuple-element.103), channel_id=1, source_target_pairs={{0,4},{4,8},{8,12},{12,16},{16,20},{20,24},{24,28},{1,5},{5,9},{9,... | collective-permute-start | bytes 196616 | tf_op jit(solution)/shard_map/ppermute | solution.py:15
  27.7 14.0 %collective-permute-start.1 = (bf16[64,512]{0,1:T(8,128)(2,1)S(1)}, bf16[64,512]{0,1:T(8,128)(2,1)S(1)}, u32[]{:S(2)}, u32[]{:S(2)}) collective-permute-start(bf16[64,512]{0,1:T(8,128)(2,1)S(1)} %get-tuple-element.104), channel_id=1, source_target_pairs={{4,0},{8,4},{12,8},{16,12},{20,16},{24,20},{28,24},{5,1},{9,5},{13... | collective-permute-start | bytes 196616 | tf_op jit(solution)/shard_map/ppermute | solution.py:18
  32.2 9.4 %all-to-all-start.3 = ((bf16[128,4,256]{0,2,1:T(8,128)(2,1)}), bf16[128,4,256]{0,2,1:T(8,128)(2,1)S(1)}, u32[]{:S(2)}, u32[]{:S(2)}) async-start(bf16[128,4,256]{0,2,1:T(8,128)(2,1)} %bitcast.14), calls=%async_computation.3 | async-start | bytes 524288 | tf_op jit(solution)/shard_map/all_to_all | solution.py:98
  35.7 14.4 %copy-start.12 = (bf16[1,128,256]{1,2,0:T(8,128)(2,1)}, bf16[1,128,256]{1,2,0:T(8,128)(2,1)S(1)}, u32[]{:S(2)}) copy-start(bf16[1,128,256]{1,2,0:T(8,128)(2,1)S(1)} %get-tuple-element.107) | copy-start | bytes 196612
  35.7 15.7 %copy-start.10 = (bf16[1,128,256]{1,2,0:T(8,128)(2,1)}, bf16[1,128,256]{1,2,0:T(8,128)(2,1)S(1)}, u32[]{:S(2)}) copy-start(bf16[1,128,256]{1,2,0:T(8,128)(2,1)S(1)} %get-tuple-element.108) | copy-start | bytes 196612
  42.3 7.9 %copy-start.7 = (bf16[256,256]{0,1:T(8,128)(2,1)}, bf16[256,256]{0,1:T(8,128)(2,1)S(1)}, u32[]{:S(2)}) copy-start(bf16[256,256]{0,1:T(8,128)(2,1)S(1)} %get-tuple-element.113) | copy-start | bytes 393220
  47.4 1.6 %copy-start.16 = (pred[128,256]{0,1:T(8,128)(4,1)S(1)}, pred[128,256]{0,1:T(8,128)(4,1)}, u32[]{:S(2)}) copy-start(pred[128,256]{0,1:T(8,128)(4,1)} %fusion.85) | copy-start | bytes 98308
  50.1 0.9 copy-start.15
  51.4 2.8 %copy-start.18 = (f32[4,128,256]{1,2,0:T(8,128)}, f32[4,128,256]{1,2,0:T(8,128)S(1)}, u32[]{:S(2)}) copy-start(f32[4,128,256]{1,2,0:T(8,128)S(1)} %get-tuple-element.122) | copy-start | bytes 1572868
  51.4 1.3 %copy-start.13 = (bf16[1,128,256]{1,2,0:T(8,128)(2,1)S(1)}, bf16[1,128,256]{1,2,0:T(8,128)(2,1)}, u32[]{:S(2)}) copy-start(bf16[1,128,256]{1,2,0:T(8,128)(2,1)} %copy-done.12) | copy-start | bytes 196612
  52.7 1.6 %copy-start.11 = (bf16[1,128,256]{1,2,0:T(8,128)(2,1)S(1)}, bf16[1,128,256]{1,2,0:T(8,128)(2,1)}, u32[]{:S(2)}) copy-start(bf16[1,128,256]{1,2,0:T(8,128)(2,1)} %copy-done.10) | copy-start | bytes 196612
  55.3 0.9 copy-start.3
  55.3 1.0 copy-start.4
  56.3 0.9 copy-start.5
  56.3 1.0 copy-start.6
  57.3 1.6 %copy-start.8 = (bf16[256,256]{0,1:T(8,128)(2,1)S(1)}, bf16[256,256]{0,1:T(8,128)(2,1)}, u32[]{:S(2)}) copy-start(bf16[256,256]{0,1:T(8,128)(2,1)} %copy-done.7) | copy-start | bytes 393220
  57.6 9.7 %collective-permute-start.2 = (f32[64,512]{0,1:T(8,128)S(1)}, f32[64,512]{0,1:T(8,128)S(1)}, u32[]{:S(2)}, u32[]{:S(2)}) collective-permute-start(f32[64,512]{0,1:T(8,128)S(1)} %slice.256), channel_id=1, source_target_pairs={{0,4},{4,8},{8,12},{12,16},{16,20},{20,24},{24,28},{1,5},{5,9},{9,... | collective-permute-start | bytes 393224 | tf_op jit(solution)/shard_map/ppermute | solution.py:26
  67.5 12.9 %collective-permute-start.3 = (f32[64,512]{0,1:T(8,128)S(1)}, f32[64,512]{0,1:T(8,128)S(1)}, u32[]{:S(2)}, u32[]{:S(2)}) collective-permute-start(f32[64,512]{0,1:T(8,128)S(1)} %get-tuple-element.91), channel_id=1, source_target_pairs={{4,0},{8,4},{12,8},{16,12},{20,16},{24,20},{28,24},{5,1},{9,5},{13... | collective-permute-start | bytes 393224 | tf_op jit(solution)/shard_map/ppermute | solution.py:26
  73.3 0.8 copy-start.9
  73.3 0.9 copy-start.14
  75.0 9.4 %all-to-all-start.4 = ((bf16[4,128,256]{2,1,0:T(8,128)(2,1)}), bf16[4,128,256]{2,1,0:T(8,128)(2,1)S(1)}, u32[]{:S(2)}, u32[]{:S(2)}) async-start(bf16[4,128,256]{2,1,0:T(8,128)(2,1)} %bitcast.42), calls=%async_computation.4 | async-start | bytes 524288 | tf_op jit(solution)/shard_map/all_to_all | solution.py:113
  84.5 9.4 %all-to-all-start.5 = ((bf16[4,128,256]{2,1,0:T(8,128)(2,1)}), bf16[4,128,256]{2,1,0:T(8,128)(2,1)S(1)}, u32[]{:S(2)}, u32[]{:S(2)}) async-start(bf16[4,128,256]{2,1,0:T(8,128)(2,1)} %bitcast.61), calls=%async_computation.5 | async-start | bytes 524288 | tf_op jit(solution)/shard_map/all_to_all | solution.py:116
  93.9 9.4 %all-to-all-start.6 = ((bf16[4,128,256]{1,2,0:T(8,128)(2,1)}), bf16[4,128,256]{1,2,0:T(8,128)(2,1)S(1)}, u32[]{:S(2)}, u32[]{:S(2)}) async-start(bf16[4,128,256]{1,2,0:T(8,128)(2,1)} %pad_maximum_fusion.1), calls=%async_computation.6 | async-start | bytes 524288 | tf_op jit(solution)/shard_map/all_to_all | solution.py:124
